TPU v7x, 512 devices: a whole 4x8x8 slice. The times are simulated.
512 devices in a mesh: expert: 64 (over x, z, core), dp: 8 (over y).
Axes of the slice: x: 4, y: 8, z: 8, core: 2. Of those that a mesh axis runs over, the one named last changes fastest.
Arguments:
- tokens: bfloat16 [65536, 2048], P(('expert', 'dp')), may hold values from -6 to 6
- upstream: bfloat16 [65536, 2048], P(('expert', 'dp')), may hold values from -6 to 6
- expert_ids: int32 [65536, 2], P(('expert', 'dp')), may hold values from 0 to 63, all different within a row; in each aligned block of 128 rows (0 to 127, 128 to 255, ...) at most 8 rows name the same one
- route_weight: bfloat16 [65536, 2], P(('expert', 'dp')), may hold values from 0.099609375 to 1
- placement: int32 [64], replicated, may hold values from 0 to 63, each once
- swap_pair: int32 [32], replicated, may hold values 0 or 1
- expert_state: bfloat16 [64, 2048, 1024], P('expert', 'dp'), may hold values from -0.125 to 0.125
- first_moment: bfloat16 [64, 2048, 1024], P('expert', 'dp'), may hold values from -60 to 60
- second_moment: bfloat16 [64, 2048, 1024], P('expert', 'dp'), may hold values from 10 to 1000
Outputs:
- token_grad: bfloat16 [65536, 2048], P(('expert', 'dp'))
- weight_grad: bfloat16 [65536, 2], P(('expert', 'dp'))
- new_state: bfloat16 [64, 2048, 1024], P('expert', 'dp')
- new_first: bfloat16 [64, 2048, 1024], P('expert', 'dp')
- new_second: bfloat16 [64, 2048, 1024], P('expert', 'dp')
Inputs may be any that keep to these rules, and one draw needn't show every extreme that they name: `expert_ids`: among the rows of one device no expert is named by more than 8 routes, and some expert reaches 8; a token's 2 experts differ.
All inputs are finite; a program needn't handle non-finite values.
Results may differ from a plain program's by a relative error of at most 0.0075.
Values may be sent and summed in bfloat16 or wider, within the bound.
A program may use at most 64 MiB of HBM per device.

v0:
```python
import math
import jax
import jax.numpy as jnp
from jax import lax
from jax.sharding import PartitionSpec as P

corr_one = 1.0 - math.exp(1000.0 * math.log(0.9))
corr_two = 1.0 - math.exp(1000.0 * math.log(0.999))


def partner_2(value, axis, stride):
    mask = 2**stride
    pairs = [(source, source ^ mask) for source in range(lax.axis_size(axis))]
    return lax.ppermute(value, axis, pairs)


def silu_grad(value):
    sig = jax.nn.sigmoid(value)
    return sig * (1.0 + value * (1.0 - sig))


def trade_state(stacked, own_flag):
    lanes_count = lax.axis_size("expert")
    partner = partner_2(stacked, "expert", lanes_count.bit_length() - 2)
    return jnp.where(own_flag == 1, partner, stacked)


def adam_update(weights, first, second, grad):
    m_next = 0.9 * first.astype(jnp.float32) + 0.1 * grad
    v_next = 0.999 * second.astype(jnp.float32) + 0.001 * grad * grad
    update = m_next / corr_one / (jnp.sqrt(v_next / corr_two) + 1e-08)
    w_old = weights.astype(jnp.float32)
    w_next = w_old - 0.001 * (update + 0.1 * w_old)
    return jnp.stack(
        [w_next.astype(jnp.bfloat16), m_next.astype(jnp.bfloat16), v_next.astype(jnp.bfloat16)]
    )


def shards(
    tokens,
    upstream,
    expert_ids,
    route_weight,
    placement,
    swap_pair,
    expert_state,
    first_moment,
    second_moment,
):
    f32 = jnp.float32
    bf16 = jnp.bfloat16
    lanes_count = lax.axis_size("expert")
    half = lanes_count // 2
    rows = tokens.shape[0]
    top = expert_ids.shape[1]
    width = tokens.shape[1]
    hidden_units = expert_state.shape[2] // 2
    capacity = 2 * rows * top // lanes_count
    halves = jnp.arange(half, dtype=jnp.int32)
    lanes = jnp.arange(lanes_count, dtype=jnp.int32)
    own_index = lax.axis_index("expert")
    own_flag = jnp.sum(jnp.where(halves == own_index % half, swap_pair, 0))
    stacked = jnp.stack([expert_state, first_moment, second_moment])
    match_half = (placement % half)[:, None] == halves[None, :]
    moved = jnp.sum(jnp.where(match_half, swap_pair[None, :], 0), 1)
    home = jnp.where(moved == 1, placement ^ half, placement)
    stacked = trade_state(stacked, own_flag)
    flat_ids = expert_ids.reshape(-1)
    match_expert = flat_ids[:, None] == lanes[None, :]
    dest = jnp.sum(jnp.where(match_expert, home[None, :], 0), 1)
    dest_hot = (dest[:, None] == lanes[None, :]).astype(jnp.int32)
    earlier = jnp.cumsum(dest_hot, 0) - dest_hot
    slot = jnp.sum(earlier * dest_hot, 1)
    position = dest * capacity + slot
    x_buf = (
        jnp.zeros((lanes_count * capacity, width), bf16)
        .at[position]
        .set(jnp.repeat(tokens, top, axis=0))
    )
    y_buf = (
        jnp.zeros((lanes_count * capacity, width), bf16)
        .at[position]
        .set(jnp.repeat(upstream, top, axis=0))
    )
    w_buf = jnp.zeros((lanes_count * capacity,), bf16).at[position].set(route_weight.reshape(-1))
    x_buf = x_buf.reshape(lanes_count, capacity, width)
    y_buf = y_buf.reshape(lanes_count, capacity, width)
    w_buf = w_buf.reshape(lanes_count, capacity)
    x_recv, y_recv, w_recv = (
        lax.all_to_all(x_buf, "expert", split_axis=0, concat_axis=0, tiled=True),
        lax.all_to_all(y_buf, "expert", split_axis=0, concat_axis=0, tiled=True),
        lax.all_to_all(w_buf, "expert", split_axis=0, concat_axis=0, tiled=True),
    )
    full = lax.all_gather(stacked[0], "dp", axis=1, tiled=True)[0]
    w_up = full[:, :hidden_units]
    w_down = full[:, hidden_units:]
    x_rows = x_recv.reshape(-1, width)
    hid = jnp.dot(x_rows, w_up, preferred_element_type=f32)
    act = jax.nn.silu(hid).astype(bf16)
    out = lax.dot_general(act, w_down, (((1,), (1,)), ((), ())), preferred_element_type=f32)
    y_rows = y_recv.reshape(-1, width)
    slot_dw = jnp.sum(y_rows.astype(f32) * out, 1).astype(bf16)
    grad_rows = (w_recv.reshape(-1)[:, None].astype(f32) * y_rows.astype(f32)).astype(bf16)
    back = jnp.dot(grad_rows, w_down, preferred_element_type=f32)
    dh = (back * silu_grad(hid)).astype(bf16)
    slot_dx = lax.dot_general(
        dh, w_up, (((1,), (1,)), ((), ())), preferred_element_type=f32
    ).astype(bf16)
    returned_dx, returned_dw = (
        lax.all_to_all(
            slot_dx.reshape(lanes_count, capacity, width),
            "expert",
            split_axis=0,
            concat_axis=0,
            tiled=True,
        ),
        lax.all_to_all(
            slot_dw.reshape(lanes_count, capacity),
            "expert",
            split_axis=0,
            concat_axis=0,
            tiled=True,
        ),
    )
    route_dx = returned_dx.reshape(-1, width)[position]
    token_grad = jnp.sum(route_dx.reshape(rows, top, width).astype(f32), 1).astype(bf16)
    weight_grad = returned_dw.reshape(-1)[position].reshape(rows, top)
    up_part = lax.dot_general(x_rows, dh, (((0,), (0,)), ((), ())), preferred_element_type=f32)
    down_part = lax.dot_general(
        grad_rows, act, (((0,), (0,)), ((), ())), preferred_element_type=f32
    )
    grad = lax.psum_scatter(
        jnp.concatenate([up_part, down_part], 1).astype(jnp.bfloat16),
        "dp",
        scatter_dimension=0,
        tiled=True,
    ).astype(jnp.float32)[None]
    updated = adam_update(stacked[0], stacked[1], stacked[2], grad)
    return (token_grad, weight_grad, updated[0], updated[1], updated[2])


def solution(mesh):
    in_specs = (
        P(("expert", "dp"), None),
        P(("expert", "dp"), None),
        P(("expert", "dp"), None),
        P(("expert", "dp"), None),
        P(),
        P(),
        P("expert", "dp", None),
        P("expert", "dp", None),
        P("expert", "dp", None),
    )
    out_specs = (
        P(("expert", "dp"), None),
        P(("expert", "dp"), None),
        P("expert", "dp", None),
        P("expert", "dp", None),
        P("expert", "dp", None),
    )
    return jax.shard_map(shards, mesh=mesh, in_specs=in_specs, out_specs=out_specs, check_vma=False)
```

profile of v0, /device:TPU:1, one launch (start us, length us, event | category | flops | bytes accessed | tf_op | source)
XLA Modules:
  0.0 280.3 jit_solution(14328996724233734354)
XLA Ops:
  7.2 1.3 copy.46
  8.5 1.2 copy.47
  9.7 0.0 copy-start.7
  9.8 0.2 copy.48
  10.0 1.3 pad_maximum_fusion.1
  11.3 5.5 %collective-permute-start = (bf16[3,1,256,1024]{2,3,1,0:T(8,128)(2,1)}, bf16[3,1,256,1024]{2,3,1,0:T(8,128)(2,1)}, u32[]{:S(2)}, u32[]{:S(2)}) collective-permute-start(bf16[3,1,256,1024]{2,3,1,0:T(8,128)(2,1)} %pad_maximum_fusion.1), channel_id=1, source_target_pairs={{0,256},{8,264},{16,272},{24,280},{32,288},{40,296},{48,304},{56,3... | collective-permute-start | bytes 4718600 | tf_op jit(solution)/shard_map/ppermute | solution.py:14
  16.8 0.1 copy.44
  17.0 0.1 reshape.189
  17.1 0.1 copy.42
  17.3 0.1 eq.70
  17.4 0.1 select_reduce_fusion.1
  17.5 0.1 select_reduce_fusion
  17.6 0.6 reduce-window.6
  18.2 0.2 slice_reduce_fusion
  18.5 0.1 fusion.35
  18.6 2.2 scatter_custom_fusion
  20.8 0.7 all_to_all.25
  21.5 12.4 %all-to-all-start = ((bf16[64,1,8]{2,1,0:T(2,128)(2,1)}), bf16[64,1,8]{2,1,0:T(2,128)(2,1)S(1)}, u32[]{:S(2)}, u32[]{:S(2)}) async-start(bf16[64,1,8]{2,1,0:T(2,128)(2,1)} %all_to_all.25), calls=%async_computation | async-start | bytes 65536 | tf_op jit(solution)/shard_map/all_to_all | solution.py:92
  33.9 0.6 broadcast_in_dim.57
  34.5 1.2 reshape.205
  35.8 4.4 %scatter_custom_fusion.2 = bf16[512,2048]{1,0:T(8,128)(2,1)} fusion(s32[256]{0:T(256)S(1)} %bitcast.87, bf16[256,2048]{1,0:T(8,128)(2,1)} %reshape.205, bf16[]{:T(256)} %constant.20.clone.1), kind=kCustom, calls=%fused_computation.37 | custom fusion | bytes 2097664 | tf_op jit(solution)/shard_map/scatter | solution.py:78
  40.2 12.2 %all-to-all-done = bf16[64,1,8]{2,1,0:T(2,128)(2,1)S(1)} async-done(((bf16[64,1,8]{2,1,0:T(2,128)(2,1)}), bf16[64,1,8]{2,1,0:T(2,128)(2,1)S(1)}, u32[]{:S(2)}, u32[]{:S(2)}) %all-to-all-start) | async-done | bytes 1056 | tf_op jit(solution)/shard_map/all_to_all | solution.py:92
  52.4 14.2 %all-to-all-start.2 = ((bf16[64,8,2048]{2,1,0:T(8,128)(2,1)}), bf16[64,8,2048]{2,1,0:T(8,128)(2,1)}, u32[]{:S(2)}, u32[]{:S(2)}) async-start(bf16[64,8,2048]{2,1,0:T(8,128)(2,1)} %bitcast.10), calls=%async_computation.2 | async-start | bytes 4194304 | tf_op jit(solution)/shard_map/all_to_all | solution.py:90
  66.6 0.2 all-gather.3.cloned.1.call-start
  66.8 0.6 fusion.37
  68.1 1.7 broadcast_select_fusion
  69.8 1.1 copy-done
  70.9 0.8 slice.34
  71.8 0.0 all-gather.3.cloned.1.call-update
  71.8 0.6 broadcast_in_dim.55
  72.4 0.4 reshape.197
  72.9 3.8 %scatter_custom_fusion.1 = bf16[512,2048]{1,0:T(8,128)(2,1)} fusion(s32[256]{0:T(256)S(1)} %bitcast.88, bf16[256,2048]{1,0:T(8,128)(2,1)S(1)} %reshape.197, bf16[]{:T(256)} %constant.20.clone.1), kind=kCustom, calls=%fused_computation.39 | custom fusion | bytes 2097154 | tf_op jit(solution)/shard_map/scatter | solution.py:83
  76.7 41.0 %all-to-all-done.2 = bf16[64,8,2048]{2,1,0:T(8,128)(2,1)} async-done(((bf16[64,8,2048]{2,1,0:T(8,128)(2,1)}), bf16[64,8,2048]{2,1,0:T(8,128)(2,1)}, u32[]{:S(2)}, u32[]{:S(2)}) %all-to-all-start.2) | async-done | bytes 2097184 | tf_op jit(solution)/shard_map/all_to_all | solution.py:90
  117.7 5.8 %all-to-all-start.1 = ((bf16[64,8,2048]{2,1,0:T(8,128)(2,1)}), bf16[64,8,2048]{2,1,0:T(8,128)(2,1)S(1)}, u32[]{:S(2)}, u32[]{:S(2)}) async-start(bf16[64,8,2048]{2,1,0:T(8,128)(2,1)} %bitcast.4), calls=%async_computation.1 | async-start | bytes 4194304 | tf_op jit(solution)/shard_map/all_to_all | solution.py:91
  123.5 0.0 reduce-scatter.2.cloned.1.call-start
  123.6 0.1 convert_reduce_fusion
  123.7 0.1 reshape.166
  123.8 10.9 %all-gather.3.cloned.1.call-done = bf16[1,1,2048,1024]{2,3,1,0:T(8,128)(2,1)} async-done(((bf16[1,1,256,1024]{2,3,1,0:T(8,128)(2,1)}), bf16[1,1,2048,1024]{2,3,1,0:T(8,128)(2,1)}) %all-gather.3.cloned.1.call-update) | async-done | bytes 4194320 | tf_op jit(solution)/shard_map/all_gather | solution.py:94
  134.7 4.5 %fusion.4 = f32[512,512]{1,0:T(8,128)} fusion(bf16[64,8,2048]{2,1,0:T(8,128)(2,1)} %all-to-all-done.2, bf16[2048,1024]{0,1:T(8,128)(2,1)} %bitcast.91), kind=kOutput, calls=%fused_computation.15 | convolution fusion | flops 1073741824 | bytes 5242880 | tf_op jit(solution)/shard_map/dot_general | solution.py:98
  139.2 35.6 %all-to-all-done.1 = bf16[64,8,2048]{2,1,0:T(8,128)(2,1)S(1)} async-done(((bf16[64,8,2048]{2,1,0:T(8,128)(2,1)}), bf16[64,8,2048]{2,1,0:T(8,128)(2,1)S(1)}, u32[]{:S(2)}, u32[]{:S(2)}) %all-to-all-start.1) | async-done | bytes 2097184 | tf_op jit(solution)/shard_map/all_to_all | solution.py:91
  174.8 3.4 %fusion.14 = bf16[512,512]{1,0:T(8,128)(2,1)S(1)} fusion(bf16[2048,1024]{0,1:T(8,128)(2,1)} %bitcast.92, f32[512,512]{1,0:T(8,128)} %fusion.4, bf16[64,8,2048]{2,1,0:T(8,128)(2,1)S(1)} %all-to-all-done.1, f32[512]{0:T(512)S(1)} %reshape.166), kind=kOutput, calls=%fused_computation.29 | convolution fusion | flops 1079246848 | bytes 5769216 | tf_op jit(solution)/shard_map/dot_general | solution.py:104
  178.2 1.5 convolution_convert_fusion
  179.7 2.9 %convolution_convert_fusion.1 = bf16[2048,512]{0,1:T(8,128)(2,1)S(1)} fusion(bf16[512,512]{1,0:T(8,128)(2,1)S(1)} %fusion.14, bf16[64,8,2048]{2,1,0:T(8,128)(2,1)} %all-to-all-done.2), kind=kOutput, calls=%fused_computation.11 | convolution fusion | flops 1074790400 | bytes 4718592 | tf_op jit(solution)/shard_map/dot_general | solution.py:128
  182.6 2.6 pad_maximum_fusion
  185.1 0.0 reduce-scatter.2.cloned.1.call-update
  185.2 3.3 %fusion.1 = bf16[512]{0:T(512)(128)(2,1)S(1)} fusion(bf16[64,8,2048]{2,1,0:T(8,128)(2,1)S(1)} %all-to-all-done.1, bf16[2048,1024]{0,1:T(8,128)(2,1)} %bitcast.93, f32[512,512]{1,0:T(8,128)} %fusion.4), kind=kOutput, calls=%fused_computation.8 | convolution fusion | flops 1078197760 | bytes 5243904 | tf_op jit(solution)/shard_map/dot_general | solution.py:100
  188.5 0.7 convert_element_type.118
  189.2 5.8 %all-to-all-start.4 = ((bf16[64,1,8]{2,1,0:T(2,128)(2,1)}), bf16[64,1,8]{2,1,0:T(2,128)(2,1)S(1)}, u32[]{:S(2)}, u32[]{:S(2)}) async-start(bf16[64,1,8]{2,1,0:T(2,128)(2,1)} %convert_element_type.118), calls=%async_computation.4 | async-start | bytes 65536 | tf_op jit(solution)/shard_map/all_to_all | solution.py:117
  195.0 4.6 %fusion.2 = bf16[64,8,2048]{2,1,0:T(8,128)(2,1)} fusion(bf16[512,512]{1,0:T(8,128)(2,1)S(1)} %fusion.14, bf16[2048,1024]{0,1:T(8,128)(2,1)} %bitcast.94), kind=kOutput, calls=%fused_computation.13 | convolution fusion | flops 1074790400 | bytes 4718592 | tf_op jit(solution)/shard_map/dot_general | solution.py:106
  199.6 4.6 %all-to-all-done.4 = bf16[64,1,8]{2,1,0:T(2,128)(2,1)S(1)} async-done(((bf16[64,1,8]{2,1,0:T(2,128)(2,1)}), bf16[64,1,8]{2,1,0:T(2,128)(2,1)S(1)}, u32[]{:S(2)}, u32[]{:S(2)}) %all-to-all-start.4) | async-done | bytes 1056 | tf_op jit(solution)/shard_map/all_to_all | solution.py:117
  204.2 5.4 %all-to-all-start.3 = ((bf16[64,8,2048]{2,1,0:T(8,128)(2,1)}), bf16[64,8,2048]{2,1,0:T(8,128)(2,1)S(1)}, u32[]{:S(2)}, u32[]{:S(2)}) async-start(bf16[64,8,2048]{2,1,0:T(8,128)(2,1)} %fusion.2), calls=%async_computation.3 | async-start | bytes 4194304 | tf_op jit(solution)/shard_map/all_to_all | solution.py:110
  209.6 0.1 reduce.3
  209.7 0.1 reshape.164
  209.8 1.9 gather_fusion.1
  211.8 0.2 reshape.165
  211.9 0.6 copy.50
  212.5 48.3 %all-to-all-done.3 = bf16[64,8,2048]{2,1,0:T(8,128)(2,1)S(1)} async-done(((bf16[64,8,2048]{2,1,0:T(8,128)(2,1)}), bf16[64,8,2048]{2,1,0:T(8,128)(2,1)S(1)}, u32[]{:S(2)}, u32[]{:S(2)}) %all-to-all-start.3) | async-done | bytes 2097184 | tf_op jit(solution)/shard_map/all_to_all | solution.py:110
  260.9 1.4 gather_fusion
  262.2 1.6 reshape.163
  263.8 4.6 %reduce_sum.61 = bf16[128,2048]{1,0:T(8,128)(2,1)} reduce(bf16[128,2,2048]{2,1,0:T(2,128)(2,1)} %reshape.163, bf16[]{:T(256)} %constant.20.clone.1), dimensions={1}, to_apply=%region_9.10 | reduce | flops 262144 | bytes 1572866 | tf_op jit(solution)/shard_map/reduce_sum | solution.py:126
  268.4 2.1 fusion.30
  270.5 1.0 copy.53
  271.5 1.0 copy.52
  272.5 1.0 copy.51
  (28 shorter events, 0.1 us)
Async XLA Ops:
  7.2 2.6 copy-start.4
  9.7 7.1 %copy-start.7 = (s32[64]{0:T(128)S(1)}, s32[64]{0:T(128)}, u32[]{:S(2)}) copy-start(s32[64]{0:T(128)} %param.13) | copy-start | bytes 772
  9.8 7.1 %copy-start.6 = (bf16[128,2]{0,1:T(2,128)(2,1)S(1)}, bf16[128,2]{0,1:T(2,128)(2,1)}, u32[]{:S(2)}) copy-start(bf16[128,2]{0,1:T(2,128)(2,1)} %param.12) | copy-start | bytes 1540
  9.8 7.4 %copy-start.5 = (s32[128,2]{0,1:T(2,128)S(1)}, s32[128,2]{0,1:T(2,128)}, u32[]{:S(2)}) copy-start(s32[128,2]{0,1:T(2,128)} %param.11) | copy-start | bytes 3076
  9.8 7.6 %copy-start.8 = (s32[32]{0:T(128)S(1)}, s32[32]{0:T(128)}, u32[]{:S(2)}) copy-start(s32[32]{0:T(128)} %param.14) | copy-start | bytes 388
  10.0 23.9 %copy-start.2 = (bf16[128,2048]{1,0:T(8,128)(2,1)S(1)}, bf16[128,2048]{1,0:T(8,128)(2,1)}, u32[]{:S(2)}) copy-start(bf16[128,2048]{1,0:T(8,128)(2,1)} %param.9) | copy-start | bytes 1572868
  11.3 56.8 %collective-permute-start = (bf16[3,1,256,1024]{2,3,1,0:T(8,128)(2,1)}, bf16[3,1,256,1024]{2,3,1,0:T(8,128)(2,1)}, u32[]{:S(2)}, u32[]{:S(2)}) collective-permute-start(bf16[3,1,256,1024]{2,3,1,0:T(8,128)(2,1)} %pad_maximum_fusion.1), channel_id=1, source_target_pairs={{0,256},{8,264},{16,272},{24,280},{32,288},{40,296},{48,304},{56,3... | collective-permute-start | bytes 4718600 | tf_op jit(solution)/shard_map/ppermute | solution.py:14
  21.5 30.9 %all-to-all-start = ((bf16[64,1,8]{2,1,0:T(2,128)(2,1)}), bf16[64,1,8]{2,1,0:T(2,128)(2,1)S(1)}, u32[]{:S(2)}, u32[]{:S(2)}) async-start(bf16[64,1,8]{2,1,0:T(2,128)(2,1)} %all_to_all.25), calls=%async_computation | async-start | bytes 65536 | tf_op jit(solution)/shard_map/all_to_all | solution.py:92
  52.4 65.3 %all-to-all-start.2 = ((bf16[64,8,2048]{2,1,0:T(8,128)(2,1)}), bf16[64,8,2048]{2,1,0:T(8,128)(2,1)}, u32[]{:S(2)}, u32[]{:S(2)}) async-start(bf16[64,8,2048]{2,1,0:T(8,128)(2,1)} %bitcast.10), calls=%async_computation.2 | async-start | bytes 4194304 | tf_op jit(solution)/shard_map/all_to_all | solution.py:90
  66.6 68.1 %all-gather.3.cloned.1.call-start = ((), (), s32[]{:S(2)}) async-start(), calls=%async_computation.7 | async-start | bytes 4718592 | tf_op jit(solution)/shard_map/all_gather | solution.py:94
  68.1 3.7 %copy-start.3 = (bf16[128,2048]{1,0:T(8,128)(2,1)S(1)}, bf16[128,2048]{1,0:T(8,128)(2,1)}, u32[]{:S(2)}) copy-start(bf16[128,2048]{1,0:T(8,128)(2,1)} %param.10) | copy-start | bytes 1572868
  69.8 1.1 copy-start
  117.7 57.1 %all-to-all-start.1 = ((bf16[64,8,2048]{2,1,0:T(8,128)(2,1)}), bf16[64,8,2048]{2,1,0:T(8,128)(2,1)S(1)}, u32[]{:S(2)}, u32[]{:S(2)}) async-start(bf16[64,8,2048]{2,1,0:T(8,128)(2,1)} %bitcast.4), calls=%async_computation.1 | async-start | bytes 4194304 | tf_op jit(solution)/shard_map/all_to_all | solution.py:91
  123.5 144.8 %reduce-scatter.2.cloned.1.call-start = ((), (), s32[]{:S(2)}) async-start(), calls=%async_computation.6 | async-start | bytes 4718592 | tf_op jit(solution)/shard_map/reduce_scatter | solution.py:132
  174.8 3.4 %copy-start.9 = (f32[512,512]{1,0:T(8,128)S(1)}, f32[512,512]{1,0:T(8,128)}, u32[]{:S(2)}) copy-start(f32[512,512]{1,0:T(8,128)} %fusion.4) | copy-start | bytes 3145732
  189.2 15.0 %all-to-all-start.4 = ((bf16[64,1,8]{2,1,0:T(2,128)(2,1)}), bf16[64,1,8]{2,1,0:T(2,128)(2,1)S(1)}, u32[]{:S(2)}, u32[]{:S(2)}) async-start(bf16[64,1,8]{2,1,0:T(2,128)(2,1)} %convert_element_type.118), calls=%async_computation.4 | async-start | bytes 65536 | tf_op jit(solution)/shard_map/all_to_all | solution.py:117
  204.2 56.7 %all-to-all-start.3 = ((bf16[64,8,2048]{2,1,0:T(8,128)(2,1)}), bf16[64,8,2048]{2,1,0:T(8,128)(2,1)S(1)}, u32[]{:S(2)}, u32[]{:S(2)}) async-start(bf16[64,8,2048]{2,1,0:T(8,128)(2,1)} %fusion.2), calls=%async_computation.3 | async-start | bytes 4194304 | tf_op jit(solution)/shard_map/all_to_all | solution.py:110
  262.2 6.2 %copy-start.1 = (bf16[3,1,256,1024]{2,3,1,0:T(8,128)(2,1)S(1)}, bf16[3,1,256,1024]{2,3,1,0:T(8,128)(2,1)}, u32[]{:S(2)}) copy-start(bf16[3,1,256,1024]{2,3,1,0:T(8,128)(2,1)} %copy-done) | copy-start | bytes 4718596
Sparse Core Ops, SparseCore 0:
  71.9 62.7 all-gather.2
  185.3 54.1 reduce-scatter.1
where the time goes:
time: 281 us; the launch traced here: 280 us
  waiting for transfers between devices  153 us (54%)
  starting transfers between devices  49.3 us (18%)
  local copies, waits for them, and re-layouts  29.1 us (10%)
  matrix products  20.2 us (7%)
  between operations  15 us (5%)
  other arithmetic  14 us (5%)
    all_to_all x1, waiting for transfers between devices, shards(): lax.all_to_all(slot_dx.reshape(lanes_count, capacity, width), 'expert', s...  48.3 us
    all_to_all x1, waiting for transfers between devices, shards(): lax.all_to_all(x_buf, 'expert', split_axis=0, concat_axis=0, tiled=True)  41 us
    all_to_all x1, waiting for transfers between devices, shards(): lax.all_to_all(y_buf, 'expert', split_axis=0, concat_axis=0, tiled=True)  35.6 us
    all_to_all x1, starting transfers between devices, shards(): lax.all_to_all(x_buf, 'expert', split_axis=0, concat_axis=0, tiled=True)  14.2 us
    all_to_all x1, starting transfers between devices, shards(): lax.all_to_all(w_buf, 'expert', split_axis=0, concat_axis=0, tiled=True)  12.4 us
    all_to_all x1, waiting for transfers between devices, shards(): lax.all_to_all(w_buf, 'expert', split_axis=0, concat_axis=0, tiled=True)  12.2 us
    all_gather x1, waiting for transfers between devices, shards(): full = lax.all_gather(stacked[0], 'dp', axis=1, tiled=True)[0]  10.9 us
    unnamed x29, local copies, waits for them, and re-layouts  7.8 us
  transfers between devices with their start and end apart: 8, of which 6 were waited for; matrix products, arithmetic and copies ran while one was open for 15% of the time, Pallas kernels for 0%

commit v1 on v0

--- a/solution.py
+++ b/solution.py
@@ -6,6 +6,19 @@
 
 corr_one = 1.0 - math.exp(1000.0 * math.log(0.9))
 corr_two = 1.0 - math.exp(1000.0 * math.log(0.999))
+
+
+def ring_gather(x, axis, dim):
+    ways = lax.axis_size(axis)
+    up = [(d, (d + 1) % ways) for d in range(ways)]
+    down = [(d, (d - 1) % ways) for d in range(ways)]
+    earlier, later = ([x], [x])
+    for _ in range(ways // 2):
+        earlier.append(lax.ppermute(earlier[-1], axis, up))
+    for _ in range((ways - 1) // 2):
+        later.append(lax.ppermute(later[-1], axis, down))
+    line = jnp.concatenate([*earlier[::-1], *later[1:]], axis=dim)
+    return jnp.roll(line, (lax.axis_index(axis) - ways // 2) * x.shape[dim], axis=dim)
 
 
 def partner_2(value, axis, stride):
@@ -91,7 +104,7 @@
         lax.all_to_all(y_buf, "expert", split_axis=0, concat_axis=0, tiled=True),
         lax.all_to_all(w_buf, "expert", split_axis=0, concat_axis=0, tiled=True),
     )
-    full = lax.all_gather(stacked[0], "dp", axis=1, tiled=True)[0]
+    full = ring_gather(stacked[0], "dp", 1)[0]
     w_up = full[:, :hidden_units]
     w_down = full[:, hidden_units:]
     x_rows = x_recv.reshape(-1, width)

time: 281 us -> 317 us (1.13); the launches traced: 280 us -> 313 us
  starting transfers between devices: 49.3 us -> 80.1 us
  local copies, waits for them, and re-layouts: 29.1 us -> 36.8 us
  waiting for transfers between devices: 153 us -> 146 us
    ppermute x1, waiting for transfers between devices: 0.01 us -> 52.7 us  [partner_2(): return lax.ppermute(value, axis, pairs)]
    all_to_all x1, waiting for transfers between devices: 41 us -> 0.01 us  [shards(): lax.all_to_all(x_buf, 'expert', split_axis=0, concat_axis=0, tiled=True)]
    ppermute x0 -> x7, waiting for transfers between devices: none -> 36.5 us  [the longest x3 22.5 us: ring_gather(): later.append(lax.ppermute(later[-1], axis, down))]
    all_to_all x1, waiting for transfers between devices: 35.6 us -> 0.01 us  [shards(): lax.all_to_all(y_buf, 'expert', split_axis=0, concat_axis=0, tiled=True)]
    ppermute x0 -> x7, starting transfers between devices: none -> 24.8 us  [the longest x3 15.7 us: ring_gather(): later.append(lax.ppermute(later[-1], axis, down))]
    all_gather x1 -> x0, waiting for transfers between devices: 10.9 us -> none  [shards(): full = lax.all_gather(stacked[0], 'dp', axis=1, tiled=True)[0]]
    all_to_all x1, waiting for transfers between devices: 12.2 us -> 3.32 us  [shards(): lax.all_to_all(w_buf, 'expert', split_axis=0, concat_axis=0, tiled=True)]
    unnamed x29 -> x44, local copies, waits for them, and re-layouts: 7.8 us -> 15 us
  transfers between devices with their start and end apart: 8 -> 14, of which waited for: 6 -> 8; matrix products, arithmetic and copies ran while one was open for 15% -> 14% of each run, Pallas kernels for 0% -> 0%
where the time goes in v1:
time: 317 us; the launch traced here: 313 us
  waiting for transfers between devices  146 us (46%)
  starting transfers between devices  80.1 us (25%)
  local copies, waits for them, and re-layouts  36.8 us (12%)
  matrix products  20.5 us (6%)
  between operations  15.3 us (5%)
  other arithmetic  14.7 us (5%)
    ppermute x1, waiting for transfers between devices, partner_2(): return lax.ppermute(value, axis, pairs)  52.7 us
    all_to_all x1, waiting for transfers between devices, shards(): lax.all_to_all(slot_dx.reshape(lanes_count, capacity, width), 'expert', s...  48.3 us
    ppermute x3, waiting for transfers between devices, ring_gather(): later.append(lax.ppermute(later[-1], axis, down))  22.5 us
    ppermute x3, starting transfers between devices, ring_gather(): later.append(lax.ppermute(later[-1], axis, down))  15.7 us
    unnamed x44, local copies, waits for them, and re-layouts  15 us
    all_to_all x1, starting transfers between devices, shards(): lax.all_to_all(w_buf, 'expert', split_axis=0, concat_axis=0, tiled=True)  14.8 us
    ppermute x4, waiting for transfers between devices, ring_gather(): earlier.append(lax.ppermute(earlier[-1], axis, up))  14 us
    all_to_all x1, starting transfers between devices, shards(): lax.all_to_all(slot_dw.reshape(lanes_count, capacity), 'expert', split_ax...  12.9 us
  transfers between devices with their start and end apart: 14, of which 8 were waited for; matrix products, arithmetic and copies ran while one was open for 14% of the time, Pallas kernels for 0%

profile of v1, /device:TPU:1, one launch (start us, length us, event | category | flops | bytes accessed | tf_op | source)
XLA Modules:
  0.0 313.1 jit_solution(14122786866334087823)
XLA Ops:
  7.2 0.8 copy.42
  8.1 0.7 and_select_fusion
  8.8 0.7 select_reduce_fusion.1
  9.5 0.7 compare_select_fusion.4
  10.3 0.6 reduce-window.6
  11.2 0.8 copy.44
  12.2 2.2 scatter_custom_fusion
  14.3 0.7 all_to_all.25
  15.1 14.8 %all-to-all-start = ((bf16[64,1,8]{2,1,0:T(2,128)(2,1)}), bf16[64,1,8]{2,1,0:T(2,128)(2,1)S(1)}, u32[]{:S(2)}, u32[]{:S(2)}) async-start(bf16[64,1,8]{2,1,0:T(2,128)(2,1)} %all_to_all.25), calls=%async_computation | async-start | bytes 65536 | tf_op jit(solution)/shard_map/all_to_all | solution.py:105
  29.9 1.7 broadcast_in_dim.57
  31.6 0.4 reshape.205
  32.1 3.7 %scatter_custom_fusion.2 = bf16[512,2048]{1,0:T(8,128)(2,1)} fusion(s32[256]{0:T(256)S(1)} %bitcast.92, bf16[256,2048]{1,0:T(8,128)(2,1)S(1)} %reshape.205, bf16[]{:T(256)} %constant.46.clone.1), kind=kCustom, calls=%fused_computation.38 | custom fusion | bytes 2097154 | tf_op jit(solution)/shard_map/scatter | solution.py:91
  35.8 3.3 %all-to-all-done = bf16[64,1,8]{2,1,0:T(2,128)(2,1)S(1)} async-done(((bf16[64,1,8]{2,1,0:T(2,128)(2,1)}), bf16[64,1,8]{2,1,0:T(2,128)(2,1)S(1)}, u32[]{:S(2)}, u32[]{:S(2)}) %all-to-all-start) | async-done | bytes 1056 | tf_op jit(solution)/shard_map/all_to_all | solution.py:105
  39.1 7.2 %all-to-all-start.2 = ((bf16[64,8,2048]{2,1,0:T(8,128)(2,1)}), bf16[64,8,2048]{2,1,0:T(8,128)(2,1)}, u32[]{:S(2)}, u32[]{:S(2)}) async-start(bf16[64,8,2048]{2,1,0:T(8,128)(2,1)} %bitcast.11), calls=%async_computation.2 | async-start | bytes 4194304 | tf_op jit(solution)/shard_map/all_to_all | solution.py:103
  46.3 0.2 copy.46
  46.6 0.2 copy.47
  47.2 4.9 %collective-permute-start = (bf16[3,1,256,1024]{2,3,1,0:T(8,128)(2,1)S(1)}, bf16[3,1,256,1024]{2,3,1,0:T(8,128)(2,1)}, u32[]{:S(2)}, u32[]{:S(2)}) collective-permute-start(bf16[3,1,256,1024]{2,3,1,0:T(8,128)(2,1)S(1)} %pad_maximum_fusion.1), channel_id=1, source_target_pairs={{0,256},{8,264},{16,272},{24,280},{32,288},{40,296},{48,304},{56,3... | collective-permute-start | bytes 4718600 | tf_op jit(solution)/shard_map/ppermute | solution.py:27
  52.1 0.6 fusion.37
  53.4 52.7 %collective-permute-done = bf16[3,1,256,1024]{2,3,1,0:T(8,128)(2,1)} collective-permute-done((bf16[3,1,256,1024]{2,3,1,0:T(8,128)(2,1)S(1)}, bf16[3,1,256,1024]{2,3,1,0:T(8,128)(2,1)}, u32[]{:S(2)}, u32[]{:S(2)}) %collective-permute-start) | collective-permute-done | bytes 1572896 | tf_op jit(solution)/shard_map/ppermute | solution.py:27
  106.1 1.6 broadcast_select_fusion
  107.8 3.2 %collective-permute-start.1 = (bf16[1,256,1024]{1,2,0:T(8,128)(2,1)S(1)}, bf16[1,256,1024]{1,2,0:T(8,128)(2,1)S(1)}, u32[]{:S(2)}, u32[]{:S(2)}) collective-permute-start(bf16[1,256,1024]{1,2,0:T(8,128)(2,1)S(1)} %slice_bitcast_fusion), channel_id=1, source_target_pairs={{0,1},{1,2},{2,3},{3,4},{4,5},{5,6},{6,7},{7,0},{8,9},{9,10},{10,1... | collective-permute-start | bytes 1572872 | tf_op jit(solution)/shard_map/ppermute | solution.py:17
  111.1 14.0 %collective-permute-done.1 = bf16[1,256,1024]{1,2,0:T(8,128)(2,1)S(1)} collective-permute-done((bf16[1,256,1024]{1,2,0:T(8,128)(2,1)S(1)}, bf16[1,256,1024]{1,2,0:T(8,128)(2,1)S(1)}, u32[]{:S(2)}, u32[]{:S(2)}) %collective-permute-start.1) | collective-permute-done | bytes 524320 | tf_op jit(solution)/shard_map/ppermute | solution.py:17
  125.0 2.1 collective-permute-start.2
  127.1 0.6 broadcast_in_dim.55
  127.8 1.2 reshape.197
  129.0 4.4 %scatter_custom_fusion.1 = bf16[512,2048]{1,0:T(8,128)(2,1)} fusion(s32[256]{0:T(256)S(1)} %bitcast.93, bf16[256,2048]{1,0:T(8,128)(2,1)} %reshape.197, bf16[]{:T(256)} %constant.46.clone.1), kind=kCustom, calls=%fused_computation.40 | custom fusion | bytes 2097664 | tf_op jit(solution)/shard_map/scatter | solution.py:96
  133.4 10.1 %all-to-all-start.1 = ((bf16[64,8,2048]{2,1,0:T(8,128)(2,1)}), bf16[64,8,2048]{2,1,0:T(8,128)(2,1)}, u32[]{:S(2)}, u32[]{:S(2)}) async-start(bf16[64,8,2048]{2,1,0:T(8,128)(2,1)} %bitcast.83), calls=%async_computation.1 | async-start | bytes 4194304 | tf_op jit(solution)/shard_map/all_to_all | solution.py:104
  143.5 4.9 %collective-permute-start.5 = (bf16[1,256,1024]{1,2,0:T(8,128)(2,1)S(1)}, bf16[1,256,1024]{1,2,0:T(8,128)(2,1)S(1)}, u32[]{:S(2)}, u32[]{:S(2)}) collective-permute-start(bf16[1,256,1024]{1,2,0:T(8,128)(2,1)S(1)} %copy-done.8), channel_id=1, source_target_pairs={{0,7},{1,0},{2,1},{3,2},{4,3},{5,4},{6,5},{7,6},{8,15},{9,8},{10,9... | collective-permute-start | bytes 1572872 | tf_op jit(solution)/shard_map/ppermute | solution.py:19
  148.4 1.9 collective-permute-start.3
  150.3 8.8 %collective-permute-done.5 = bf16[1,256,1024]{1,2,0:T(8,128)(2,1)S(1)} collective-permute-done((bf16[1,256,1024]{1,2,0:T(8,128)(2,1)S(1)}, bf16[1,256,1024]{1,2,0:T(8,128)(2,1)S(1)}, u32[]{:S(2)}, u32[]{:S(2)}) %collective-permute-start.5) | collective-permute-done | bytes 524320 | tf_op jit(solution)/shard_map/ppermute | solution.py:19
  159.1 5.4 %collective-permute-start.6 = (bf16[1,256,1024]{1,2,0:T(8,128)(2,1)S(1)}, bf16[1,256,1024]{1,2,0:T(8,128)(2,1)S(1)}, u32[]{:S(2)}, u32[]{:S(2)}) collective-permute-start(bf16[1,256,1024]{1,2,0:T(8,128)(2,1)S(1)} %collective-permute-done.5), channel_id=1, source_target_pairs={{0,7},{1,0},{2,1},{3,2},{4,3},{5,4},{6,5},{7,6},{8,15},{9,8},{10,9... | collective-permute-start | bytes 1572872 | tf_op jit(solution)/shard_map/ppermute | solution.py:19
  164.6 1.9 collective-permute-start.4
  166.7 7.8 %collective-permute-done.6 = bf16[1,256,1024]{1,2,0:T(8,128)(2,1)S(1)} collective-permute-done((bf16[1,256,1024]{1,2,0:T(8,128)(2,1)S(1)}, bf16[1,256,1024]{1,2,0:T(8,128)(2,1)S(1)}, u32[]{:S(2)}, u32[]{:S(2)}) %collective-permute-start.6) | collective-permute-done | bytes 524320 | tf_op jit(solution)/shard_map/ppermute | solution.py:19
  174.5 5.4 %collective-permute-start.7 = (bf16[1,256,1024]{1,2,0:T(8,128)(2,1)S(1)}, bf16[1,256,1024]{1,2,0:T(8,128)(2,1)S(1)}, u32[]{:S(2)}, u32[]{:S(2)}) collective-permute-start(bf16[1,256,1024]{1,2,0:T(8,128)(2,1)S(1)} %collective-permute-done.6), channel_id=1, source_target_pairs={{0,7},{1,0},{2,1},{3,2},{4,3},{5,4},{6,5},{7,6},{8,15},{9,8},{10,9... | collective-permute-start | bytes 1572872 | tf_op jit(solution)/shard_map/ppermute | solution.py:19
  179.9 1.1 constant_dynamic-update-slice_fusion.15
  181.0 1.1 constant_dynamic-update-slice_fusion.14
  182.1 1.1 constant_dynamic-update-slice_fusion.13
  183.5 5.9 %collective-permute-done.7 = bf16[1,256,1024]{1,2,0:T(8,128)(2,1)S(1)} collective-permute-done((bf16[1,256,1024]{1,2,0:T(8,128)(2,1)S(1)}, bf16[1,256,1024]{1,2,0:T(8,128)(2,1)S(1)}, u32[]{:S(2)}, u32[]{:S(2)}) %collective-permute-start.7) | collective-permute-done | bytes 524320 | tf_op jit(solution)/shard_map/ppermute | solution.py:19
  189.5 1.1 constant_dynamic-update-slice_fusion.7
  190.7 1.1 constant_dynamic-update-slice_fusion.6
  191.8 1.1 constant_dynamic-update-slice_fusion.5
  193.3 0.3 dynamic-slice_bitcast_fusion
  193.6 2.0 copy-done.2
  195.6 2.9 fusion.4
  198.5 3.7 %fusion.14 = bf16[512,512]{1,0:T(8,128)(2,1)S(1)} fusion(bf16[2048,1024]{0,1:T(8,128)(2,1)} %copy-done.2, f32[512,512]{1,0:T(8,128)S(1)} %fusion.4, bf16[64,8,2048]{2,1,0:T(8,128)(2,1)} %all-to-all-done.1, f32[512]{0:T(512)S(1)} %reshape.166), kind=kOutput, calls=%fused_computation.30 | convolution fusion | flops 1079246848 | bytes 5769216 | tf_op jit(solution)/shard_map/dot_general | solution.py:117
  202.2 3.1 convolution_convert_fusion
  205.2 2.9 convolution_convert_fusion.1
  208.1 2.5 pad_maximum_fusion
  210.6 3.6 %fusion.1 = bf16[512]{0:T(512)(128)(2,1)S(1)} fusion(bf16[64,8,2048]{2,1,0:T(8,128)(2,1)} %all-to-all-done.1, bf16[2048,1024]{0,1:T(8,128)(2,1)} %copy-done.2, f32[512,512]{1,0:T(8,128)S(1)} %fusion.4), kind=kOutput, calls=%fused_computation.8 | convolution fusion | flops 1078197760 | bytes 5243904 | tf_op jit(solution)/shard_map/dot_general | solution.py:113
  214.3 0.7 convert_element_type.118
  215.0 12.9 %all-to-all-start.4 = ((bf16[64,1,8]{2,1,0:T(2,128)(2,1)}), bf16[64,1,8]{2,1,0:T(2,128)(2,1)S(1)}, u32[]{:S(2)}, u32[]{:S(2)}) async-start(bf16[64,1,8]{2,1,0:T(2,128)(2,1)} %convert_element_type.118), calls=%async_computation.4 | async-start | bytes 65536 | tf_op jit(solution)/shard_map/all_to_all | solution.py:130
  227.9 4.3 %fusion.2 = bf16[64,8,2048]{2,1,0:T(8,128)(2,1)} fusion(bf16[512,512]{1,0:T(8,128)(2,1)S(1)} %fusion.14, bf16[2048,1024]{0,1:T(8,128)(2,1)} %copy-done.2), kind=kOutput, calls=%fused_computation.14 | convolution fusion | flops 1074790400 | bytes 4718592 | tf_op jit(solution)/shard_map/dot_general | solution.py:119
  232.2 4.9 %all-to-all-done.4 = bf16[64,1,8]{2,1,0:T(2,128)(2,1)S(1)} async-done(((bf16[64,1,8]{2,1,0:T(2,128)(2,1)}), bf16[64,1,8]{2,1,0:T(2,128)(2,1)S(1)}, u32[]{:S(2)}, u32[]{:S(2)}) %all-to-all-start.4) | async-done | bytes 1056 | tf_op jit(solution)/shard_map/all_to_all | solution.py:130
  237.1 5.4 %all-to-all-start.3 = ((bf16[64,8,2048]{2,1,0:T(8,128)(2,1)}), bf16[64,8,2048]{2,1,0:T(8,128)(2,1)S(1)}, u32[]{:S(2)}, u32[]{:S(2)}) async-start(bf16[64,8,2048]{2,1,0:T(8,128)(2,1)} %fusion.2), calls=%async_computation.3 | async-start | bytes 4194304 | tf_op jit(solution)/shard_map/all_to_all | solution.py:123
  242.7 1.9 gather_fusion.1
  244.8 0.6 copy.50
  245.4 48.3 %all-to-all-done.3 = bf16[64,8,2048]{2,1,0:T(8,128)(2,1)S(1)} async-done(((bf16[64,8,2048]{2,1,0:T(8,128)(2,1)}), bf16[64,8,2048]{2,1,0:T(8,128)(2,1)S(1)}, u32[]{:S(2)}, u32[]{:S(2)}) %all-to-all-start.3) | async-done | bytes 2097184 | tf_op jit(solution)/shard_map/all_to_all | solution.py:123
  293.7 1.4 gather_fusion
  295.1 1.5 reshape.163
  296.6 4.6 %reduce_sum.61 = bf16[128,2048]{1,0:T(8,128)(2,1)} reduce(bf16[128,2,2048]{2,1,0:T(2,128)(2,1)} %reshape.163, bf16[]{:T(256)} %constant.46.clone.1), dimensions={1}, to_apply=%region_9.10 | reduce | flops 262144 | bytes 1572866 | tf_op jit(solution)/shard_map/reduce_sum | solution.py:139
  301.2 2.1 fusion.30
  303.2 1.0 copy.51
  304.3 1.0 copy.52
  305.3 1.0 copy.53
  (56 shorter events, 2.5 us)
Async XLA Ops:
  15.1 24.1 %all-to-all-start = ((bf16[64,1,8]{2,1,0:T(2,128)(2,1)}), bf16[64,1,8]{2,1,0:T(2,128)(2,1)S(1)}, u32[]{:S(2)}, u32[]{:S(2)}) async-start(bf16[64,1,8]{2,1,0:T(2,128)(2,1)} %all_to_all.25), calls=%async_computation | async-start | bytes 65536 | tf_op jit(solution)/shard_map/all_to_all | solution.py:105
  31.6 14.7 %copy-start.4 = (bf16[1,256,1024]{2,1,0:T(8,128)(2,1)S(1)}, bf16[1,256,1024]{2,1,0:T(8,128)(2,1)}, u32[]{:S(2)}) copy-start(bf16[1,256,1024]{2,1,0:T(8,128)(2,1)} %param.15) | copy-start | bytes 1572868
  32.0 14.5 %copy-start.5 = (bf16[1,256,1024]{2,1,0:T(8,128)(2,1)S(1)}, bf16[1,256,1024]{2,1,0:T(8,128)(2,1)}, u32[]{:S(2)}) copy-start(bf16[1,256,1024]{2,1,0:T(8,128)(2,1)} %param.16) | copy-start | bytes 1572868
  32.1 14.7 %copy-start.6 = (bf16[1,256,1024]{2,1,0:T(8,128)(2,1)S(1)}, bf16[1,256,1024]{2,1,0:T(8,128)(2,1)}, u32[]{:S(2)}) copy-start(bf16[1,256,1024]{2,1,0:T(8,128)(2,1)} %param.17) | copy-start | bytes 1572868
  39.1 94.3 %all-to-all-start.2 = ((bf16[64,8,2048]{2,1,0:T(8,128)(2,1)}), bf16[64,8,2048]{2,1,0:T(8,128)(2,1)}, u32[]{:S(2)}, u32[]{:S(2)}) async-start(bf16[64,8,2048]{2,1,0:T(8,128)(2,1)} %bitcast.11), calls=%async_computation.2 | async-start | bytes 4194304 | tf_op jit(solution)/shard_map/all_to_all | solution.py:103
  46.3 5.8 %copy-start.9 = (s32[32]{0:T(128)S(1)}, s32[32]{0:T(128)}, u32[]{:S(2)}) copy-start(s32[32]{0:T(128)} %param.14) | copy-start | bytes 388
  47.2 59.0 %collective-permute-start = (bf16[3,1,256,1024]{2,3,1,0:T(8,128)(2,1)S(1)}, bf16[3,1,256,1024]{2,3,1,0:T(8,128)(2,1)}, u32[]{:S(2)}, u32[]{:S(2)}) collective-permute-start(bf16[3,1,256,1024]{2,3,1,0:T(8,128)(2,1)S(1)} %pad_maximum_fusion.1), channel_id=1, source_target_pairs={{0,256},{8,264},{16,272},{24,280},{32,288},{40,296},{48,304},{56,3... | collective-permute-start | bytes 4718600 | tf_op jit(solution)/shard_map/ppermute | solution.py:27
  53.4 73.7 %copy-start.3 = (bf16[128,2048]{1,0:T(8,128)(2,1)S(1)}, bf16[128,2048]{1,0:T(8,128)(2,1)}, u32[]{:S(2)}) copy-start(bf16[128,2048]{1,0:T(8,128)(2,1)} %param.10) | copy-start | bytes 1572868
  107.8 85.2 %copy-start = (bf16[3,1,256,1024]{2,3,1,0:T(8,128)(2,1)}, bf16[3,1,256,1024]{2,3,1,0:T(8,128)(2,1)S(1)}, u32[]{:S(2)}) copy-start(bf16[3,1,256,1024]{2,3,1,0:T(8,128)(2,1)S(1)} %broadcast_select_fusion) | copy-start | bytes 4718596
  107.8 17.2 %copy-start.7 = (bf16[1,256,1024]{1,2,0:T(8,128)(2,1)}, bf16[1,256,1024]{1,2,0:T(8,128)(2,1)S(1)}, u32[]{:S(2)}) copy-start(bf16[1,256,1024]{1,2,0:T(8,128)(2,1)S(1)} %slice_bitcast_fusion) | copy-start | bytes 1572868
  107.8 17.2 %collective-permute-start.1 = (bf16[1,256,1024]{1,2,0:T(8,128)(2,1)S(1)}, bf16[1,256,1024]{1,2,0:T(8,128)(2,1)S(1)}, u32[]{:S(2)}, u32[]{:S(2)}) collective-permute-start(bf16[1,256,1024]{1,2,0:T(8,128)(2,1)S(1)} %slice_bitcast_fusion), channel_id=1, source_target_pairs={{0,1},{1,2},{2,3},{3,4},{4,5},{5,6},{6,7},{7,0},{8,9},{9,10},{10,1... | collective-permute-start | bytes 1572872 | tf_op jit(solution)/shard_map/ppermute | solution.py:17
  125.0 23.4 %collective-permute-start.2 = (bf16[1,256,1024]{1,2,0:T(8,128)(2,1)S(1)}, bf16[1,256,1024]{1,2,0:T(8,128)(2,1)}, u32[]{:S(2)}, u32[]{:S(2)}) collective-permute-start(bf16[1,256,1024]{1,2,0:T(8,128)(2,1)S(1)} %collective-permute-done.1), channel_id=1, source_target_pairs={{0,1},{1,2},{2,3},{3,4},{4,5},{5,6},{6,7},{7,0},{8,9},{9,10},{10,1... | collective-permute-start | bytes 1572872 | tf_op jit(solution)/shard_map/ppermute | solution.py:17
  129.0 14.5 %copy-start.8 = (bf16[1,256,1024]{1,2,0:T(8,128)(2,1)S(1)}, bf16[1,256,1024]{1,2,0:T(8,128)(2,1)}, u32[]{:S(2)}) copy-start(bf16[1,256,1024]{1,2,0:T(8,128)(2,1)} %copy-done.7) | copy-start | bytes 1572868
  133.4 65.0 %all-to-all-start.1 = ((bf16[64,8,2048]{2,1,0:T(8,128)(2,1)}), bf16[64,8,2048]{2,1,0:T(8,128)(2,1)}, u32[]{:S(2)}, u32[]{:S(2)}) async-start(bf16[64,8,2048]{2,1,0:T(8,128)(2,1)} %bitcast.83), calls=%async_computation.1 | async-start | bytes 4194304 | tf_op jit(solution)/shard_map/all_to_all | solution.py:104
  143.5 157.7 %reduce-scatter.2.cloned.1.call-start = ((), (), s32[]{:S(2)}) async-start(), calls=%async_computation.6 | async-start | bytes 4718592 | tf_op jit(solution)/shard_map/reduce_scatter | solution.py:145
  143.5 15.6 %collective-permute-start.5 = (bf16[1,256,1024]{1,2,0:T(8,128)(2,1)S(1)}, bf16[1,256,1024]{1,2,0:T(8,128)(2,1)S(1)}, u32[]{:S(2)}, u32[]{:S(2)}) collective-permute-start(bf16[1,256,1024]{1,2,0:T(8,128)(2,1)S(1)} %copy-done.8), channel_id=1, source_target_pairs={{0,7},{1,0},{2,1},{3,2},{4,3},{5,4},{6,5},{7,6},{8,15},{9,8},{10,9... | collective-permute-start | bytes 1572872 | tf_op jit(solution)/shard_map/ppermute | solution.py:19
  148.4 16.1 %collective-permute-start.3 = (bf16[1,256,1024]{1,2,0:T(8,128)(2,1)}, bf16[1,256,1024]{1,2,0:T(8,128)(2,1)}, u32[]{:S(2)}, u32[]{:S(2)}) collective-permute-start(bf16[1,256,1024]{1,2,0:T(8,128)(2,1)} %collective-permute-done.2), channel_id=1, source_target_pairs={{0,1},{1,2},{2,3},{3,4},{4,5},{5,6},{6,7},{7,0},{8,9},{9,10},{10,1... | collective-permute-start | bytes 1572872 | tf_op jit(solution)/shard_map/ppermute | solution.py:17
  159.1 15.3 %collective-permute-start.6 = (bf16[1,256,1024]{1,2,0:T(8,128)(2,1)S(1)}, bf16[1,256,1024]{1,2,0:T(8,128)(2,1)S(1)}, u32[]{:S(2)}, u32[]{:S(2)}) collective-permute-start(bf16[1,256,1024]{1,2,0:T(8,128)(2,1)S(1)} %collective-permute-done.5), channel_id=1, source_target_pairs={{0,7},{1,0},{2,1},{3,2},{4,3},{5,4},{6,5},{7,6},{8,15},{9,8},{10,9... | collective-permute-start | bytes 1572872 | tf_op jit(solution)/shard_map/ppermute | solution.py:19
  164.6 15.3 %collective-permute-start.4 = (bf16[1,256,1024]{1,2,0:T(8,128)(2,1)}, bf16[1,256,1024]{1,2,0:T(8,128)(2,1)}, u32[]{:S(2)}, u32[]{:S(2)}) collective-permute-start(bf16[1,256,1024]{1,2,0:T(8,128)(2,1)} %collective-permute-done.3), channel_id=1, source_target_pairs={{0,1},{1,2},{2,3},{3,4},{4,5},{5,6},{6,7},{7,0},{8,9},{9,10},{10,1... | collective-permute-start | bytes 1572872 | tf_op jit(solution)/shard_map/ppermute | solution.py:17
  174.5 15.0 %collective-permute-start.7 = (bf16[1,256,1024]{1,2,0:T(8,128)(2,1)S(1)}, bf16[1,256,1024]{1,2,0:T(8,128)(2,1)S(1)}, u32[]{:S(2)}, u32[]{:S(2)}) collective-permute-start(bf16[1,256,1024]{1,2,0:T(8,128)(2,1)S(1)} %collective-permute-done.6), channel_id=1, source_target_pairs={{0,7},{1,0},{2,1},{3,2},{4,3},{5,4},{6,5},{7,6},{8,15},{9,8},{10,9... | collective-permute-start | bytes 1572872 | tf_op jit(solution)/shard_map/ppermute | solution.py:19
  193.6 2.0 copy-start.2
  215.0 22.1 %all-to-all-start.4 = ((bf16[64,1,8]{2,1,0:T(2,128)(2,1)}), bf16[64,1,8]{2,1,0:T(2,128)(2,1)S(1)}, u32[]{:S(2)}, u32[]{:S(2)}) async-start(bf16[64,1,8]{2,1,0:T(2,128)(2,1)} %convert_element_type.118), calls=%async_computation.4 | async-start | bytes 65536 | tf_op jit(solution)/shard_map/all_to_all | solution.py:130
  237.1 56.6 %all-to-all-start.3 = ((bf16[64,8,2048]{2,1,0:T(8,128)(2,1)}), bf16[64,8,2048]{2,1,0:T(8,128)(2,1)S(1)}, u32[]{:S(2)}, u32[]{:S(2)}) async-start(bf16[64,8,2048]{2,1,0:T(8,128)(2,1)} %fusion.2), calls=%async_computation.3 | async-start | bytes 4194304 | tf_op jit(solution)/shard_map/all_to_all | solution.py:123
  295.1 6.1 %copy-start.1 = (bf16[3,1,256,1024]{2,3,1,0:T(8,128)(2,1)S(1)}, bf16[3,1,256,1024]{2,3,1,0:T(8,128)(2,1)}, u32[]{:S(2)}) copy-start(bf16[3,1,256,1024]{2,3,1,0:T(8,128)(2,1)} %copy-done) | copy-start | bytes 4718596
Sparse Core Ops, SparseCore 0:
  210.8 61.8 reduce-scatter.1
